TPU v7x, 256 devices: a whole 4x4x8 slice. The times are simulated.
256 devices in a mesh: elec: 16 (over z_hi, x, core), space: 16 (over z_lo, y).
Axes of the slice: x: 4, y: 4, z: 8 (z_hi: 2, z_lo: 4; z = z_hi * 4 + z_lo), core: 2. Of those that a mesh axis runs over, the one named last changes fastest.
Arguments:
- potentials: bfloat16 [2048, 32, 8, 128], P('elec', 'space'), may hold values from -6 to 6
- quadrupoles: int32 [4, 32768], replicated, may hold values from 0 to 2047
- residuals: float32 [32768], replicated, may hold values from -0.03125 to 0.03125
- cell_weight: float32 [32, 8, 128], P('space'), may hold values from 0.5 to 2
Outputs:
- model_gradient: float32 [32, 8, 128], P('space')
All inputs are finite; a program needn't handle non-finite values.
Results may differ from a plain program's by a relative error of at most 0.0054.
Values may be sent and summed in bfloat16 or wider, within the bound.
A program may use at most 192 MiB of HBM per device.

v0:
```python
import jax
import jax.numpy as jnp
from jax import lax
from jax.sharding import PartitionSpec as P


def extended(block, sides, width):
    for axis, dim in sides:
        count = lax.axis_size(axis)
        forward = [(i, i + 1) for i in range(count - 1)]
        backward = [(target, source) for source, target in forward]
        low = lax.ppermute(
            lax.slice_in_dim(block, block.shape[dim] - width, None, axis=dim), axis, forward
        )
        high = lax.ppermute(lax.slice_in_dim(block, 0, width, axis=dim), axis, backward)
        block = jnp.concatenate([low, block, high], axis=dim)
    return block


def slopes_of(padded):
    field = padded.astype(jnp.float32)
    grad_x = 0.5 * (field[:, 2:] - field[:, :-2])
    inner = field[:, 1:-1]
    pad_z = jnp.pad(inner, ((0, 0), (0, 0), (1, 1), (0, 0)))
    grad_z = 0.5 * (pad_z[:, :, 2:] - pad_z[:, :, :-2])
    pad_y = jnp.pad(inner, ((0, 0), (0, 0), (0, 0), (1, 1)))
    grad_y = 0.5 * (pad_y[:, :, :, 2:] - pad_y[:, :, :, :-2])
    return jnp.stack([grad_x, grad_z, grad_y], axis=0).astype(jnp.bfloat16)


def coupling_rows(quadrupoles, residuals, first, count, width):
    source_a = quadrupoles[0]
    source_b = quadrupoles[1]
    probe_m = quadrupoles[2]
    probe_n = quadrupoles[3]
    rows = jnp.concatenate([source_a, source_a, source_b, source_b]) - first
    cols = jnp.concatenate([probe_m, probe_n, probe_m, probe_n])
    values = jnp.concatenate([residuals, -residuals, -residuals, residuals])
    valid = (rows >= 0) & (rows < count)
    flat = jnp.where(valid, rows * width + cols, count * width)
    summed = jax.ops.segment_sum(values, flat, num_segments=count * width)
    return summed.reshape(count, width).astype(jnp.bfloat16)


def local(potentials, quadrupoles, residuals, cell_weight):
    local_fields, planes_dev, thickness, breadth = potentials.shape
    groups = lax.axis_size("elec")
    width = local_fields * groups
    cells = planes_dev * thickness * breadth
    padded = extended(potentials, (("space", 1),), 1)
    own_slopes = slopes_of(padded)
    first = lax.axis_index("elec") * local_fields
    coupling = coupling_rows(quadrupoles, residuals, first, local_fields, width)
    piece = lax.all_gather(padded, "elec", axis=0, tiled=True)
    count = piece.shape[0]
    part = slopes_of(piece).reshape(3, count, cells)
    image = jnp.einsum("ef,kfc->kec", coupling, part, preferred_element_type=jnp.float32)
    partial_value = jnp.sum(
        own_slopes.reshape(3, local_fields, cells).astype(jnp.float32) * image, axis=(0, 1)
    )
    summed = lax.psum(partial_value, "elec").reshape(planes_dev, thickness, breadth)
    return summed * cell_weight


def solution(mesh):
    placed = (P("elec", "space", None, None), P(), P(), P("space", None, None))
    return jax.shard_map(
        local, mesh=mesh, in_specs=placed, out_specs=P("space", None, None), check_vma=False
    )
```

profile of v0, /device:TPU:32, one launch (start us, length us, event | category | flops | bytes accessed | tf_op | source)
XLA Modules:
  0.0 904.9 jit_solution(13923487650861097079)
XLA Ops:
  6.5 0.0 all-gather.2.cloned.1.call-start
  6.5 1.1 fusion.28
  7.6 3.5 collective-permute-start
  11.1 4.5 collective-permute-start.1
  15.6 4.1 collective-permute-done
  19.7 1.1 constant_dynamic-update-slice_fusion.1
  20.8 0.0 collective-permute-done.1
  20.8 0.1 constant_dynamic-update-slice_fusion
  20.9 0.0 copy-start
  20.9 1.0 copy-done
  21.9 0.0 all-gather.2.cloned.1.call-update
  21.9 0.9 neg.4
  22.8 1.0 pad_maximum_fusion
  23.8 2.4 slice_bitcast_fusion.3
  26.2 5.3 and_select_fusion
  31.6 682.8 %scatter_custom_fusion = f32[262144]{0:T(1024)S(1)} fusion(s32[131072]{0:T(1024)S(1)} %bitcast.27, f32[131072]{0:T(1024)S(1)} %pad_maximum_fusion, f32[]{:T(128)} %constant.9.clone.1), kind=kCustom, calls=%fused_computation.39 | custom fusion | flops 131072 | bytes 1048580 | tf_op jit(solution)/shard_map/scatter-add | solution.py:41
  714.4 0.1 convert_element_type.30
  714.5 1.0 reshape.167
  715.5 1.1 slice.82
  716.6 1.5 convert_element_type.27
  718.1 0.8 fusion.19
  718.9 1.0 stack.25
  720.0 0.2 stack.26
  720.2 0.1 fusion.24
  720.3 0.2 stack.24
  720.6 0.0 all-gather.2.cloned.1.call-done
  720.6 9.6 %slice.85 = f32[2048,2,8,128]{3,2,1,0:T(8,128)} slice(bf16[2048,4,8,128]{3,2,1,0:T(8,128)(2,1)} %all-gather.2.cloned.1.call-done), slice={[0:2048], [1:3], [0:8], [0:128]} | slice | bytes 33554432 | tf_op jit(solution)/shard_map/slice | solution.py:23
  730.2 33.1 %fusion.8 = (bf16[2048,2,8,128]{3,2,1,0:T(8,128)(2,1)}, bf16[2048,2,8,128]{3,2,1,0:T(8,128)(2,1)}) fusion(f32[2048,2,8,128]{3,2,1,0:T(8,128)} %slice.85), kind=kLoop, calls=%fused_computation.13 | loop fusion | flops 25165824 | bytes 33554432 | tf_op jit(solution)/shard_map/convert.4
  763.3 13.3 %stack.29 = bf16[1,2048,2048]{2,1,0:T(8,128)(2,1)} reshape(bf16[2048,2,8,128]{3,2,1,0:T(8,128)(2,1)} %get-tuple-element.5) | data formatting | bytes 16777216 | tf_op jit(solution)/shard_map/stack | solution.py:28
  776.6 13.3 %stack.30 = bf16[1,2048,2048]{2,1,0:T(8,128)(2,1)} reshape(bf16[2048,2,8,128]{3,2,1,0:T(8,128)(2,1)} %get-tuple-element.6) | data formatting | bytes 16777216 | tf_op jit(solution)/shard_map/stack | solution.py:28
  789.9 18.8 %convert_element_type.29 = f32[2048,4,8,128]{3,2,1,0:T(8,128)} convert(bf16[2048,4,8,128]{3,2,1,0:T(8,128)(2,1)} %all-gather.2.cloned.1.call-done) | non-fusion elementwise | flops 8388608 | bytes 50331648 | tf_op jit(solution)/shard_map/convert_element_type | solution.py:21
  808.7 15.1 %fusion.13 = bf16[2048,2,8,128]{3,2,1,0:T(8,128)(2,1)} fusion(f32[2048,4,8,128]{3,2,1,0:T(8,128)} %convert_element_type.29), kind=kLoop, calls=%fused_computation.19 | loop fusion | flops 12582912 | bytes 41943040 | tf_op jit(solution)/shard_map/convert.5
  823.8 0.0 copy-start.1
  823.8 0.0 copy-start.2
  823.8 13.4 %stack.28 = bf16[1,2048,2048]{2,1,0:T(8,128)(2,1)} reshape(bf16[2048,2,8,128]{3,2,1,0:T(8,128)(2,1)} %fusion.13) | data formatting | bytes 16777216 | tf_op jit(solution)/shard_map/stack | solution.py:28
  837.2 0.0 copy-done.1
  837.2 0.0 copy-done.2
  837.2 0.0 copy-start.3
  837.2 9.9 %fusion.14 = f32[2048]{0:T(1024)S(1)} fusion(bf16[128,2048,1]{1,0,2:T(8,128)(2,1)S(1)} %copy-done.1, bf16[1,2048,2048]{2,1,0:T(8,128)(2,1)} %stack.30, bf16[1,2048,2048]{2,1,0:T(8,128)(2,1)} %stack.29, bf16[1,2048,2048]{2,1,0:T(8,128)(2,1)} %stack.28, bf16[1,128,2048]{2,1,0:T(8,128)(2,1)S(1)} %stack.26, bf16[1,128,2048]{2,1,0:T(8,128)(2,1)S(1)} %copy-done.2, ...), kind=kOutput, calls=%fused_computation.21 | convolution fusion | flops 3300653056 | bytes 27271168 | tf_op jit(solution)/shard_map/ef,kfc->kec/dot_general | solution.py:57
  847.1 50.3 %psum.7 = f32[2,8,128]{2,1,0:T(8,128)S(1)} all-reduce(f32[2,8,128]{2,1,0:T(8,128)S(1)} %bitcast.28), channel_id=1, replica_groups=mesh['elec'=16,'space'=16] {'elec'}, use_global_device_ids=true, to_apply=%region_2.3 | all-reduce | flops 2048 | bytes 16384 | tf_op jit(solution)/shard_map/psum | solution.py:61
  897.4 0.0 copy-done.3
  897.5 0.6 mul.50
  (1 shorter events, 0.0 us)
Async XLA Ops:
  6.5 714.1 %all-gather.2.cloned.1.call-start = ((), (), s32[]{:S(2)}) async-start(), calls=%async_computation | async-start | bytes 17825792 | tf_op jit(solution)/shard_map/all_gather | solution.py:54
  7.6 12.0 %collective-permute-start = (bf16[128,1,8,128]{3,2,1,0:T(8,128)(2,1)S(1)}, bf16[128,1,8,128]{3,2,1,0:T(8,128)(2,1)S(1)}, u32[]{:S(2)}, u32[]{:S(2)}) collective-permute-start(bf16[128,1,8,128]{3,2,1,0:T(8,128)(2,1)S(1)} %get-tuple-element.10), channel_id=1, source_target_pairs={{0,1},{1,2},{2,3},{3,4},{4,5},{5,6},{6,7},{7,8},{8,9},{9,10},{10,1... | collective-permute-start | bytes 786440 | tf_op jit(solution)/shard_map/ppermute | solution.py:12
  11.1 9.7 %collective-permute-start.1 = (bf16[128,1,8,128]{3,2,1,0:T(8,128)(2,1)S(1)}, bf16[128,1,8,128]{3,2,1,0:T(8,128)(2,1)S(1)}, u32[]{:S(2)}, u32[]{:S(2)}) collective-permute-start(bf16[128,1,8,128]{3,2,1,0:T(8,128)(2,1)S(1)} %get-tuple-element.9), channel_id=1, source_target_pairs={{1,0},{2,1},{3,2},{4,3},{5,4},{6,5},{7,6},{8,7},{9,8},{10,9},{11,1... | collective-permute-start | bytes 786440 | tf_op jit(solution)/shard_map/ppermute | solution.py:15
  20.9 1.0 copy-start
  823.8 13.4 %copy-start.1 = (bf16[128,2048,1]{1,0,2:T(8,128)(2,1)S(1)}, bf16[128,2048,1]{1,0,2:T(8,128)(2,1)}, u32[]{:S(2)}) copy-start(bf16[128,2048,1]{1,0,2:T(8,128)(2,1)} %reshape.167) | copy-start | bytes 1572868
  823.8 13.4 %copy-start.2 = (bf16[1,128,2048]{2,1,0:T(8,128)(2,1)S(1)}, bf16[1,128,2048]{2,1,0:T(8,128)(2,1)}, u32[]{:S(2)}) copy-start(bf16[1,128,2048]{2,1,0:T(8,128)(2,1)} %stack.25) | copy-start | bytes 1572868
  837.2 60.2 %copy-start.3 = (f32[2,8,128]{2,1,0:T(8,128)S(1)}, f32[2,8,128]{2,1,0:T(8,128)}, u32[]{:S(2)}) copy-start(f32[2,8,128]{2,1,0:T(8,128)} %param.7) | copy-start | bytes 24580
Sparse Core Ops, SparseCore 0:
  22.0 176.5 all-gather.1
where the time goes:
time: 908 us; the launch traced here: 905 us
  other arithmetic  760 us (84%)
  local copies, waits for them, and re-layouts  58.9 us (6%)
  blocking collectives  50.3 us (6%)
  between operations  13.6 us (1%)
  matrix products  9.86 us (1%)
    scatter-add x1, other arithmetic, coupling_rows(): summed = jax.ops.segment_sum(values, flat, num_segments=count * width)  683 us
    psum x1, blocking collectives, local(): lax.psum(partial_value, 'elec').reshape(planes_dev, thickness, breadth)  50.3 us
    another operation x4, other arithmetic  49.1 us
    another operation x6, local copies, waits for them, and re-layouts, slopes_of(): return jnp.stack([grad_x, grad_z, grad_y], axis=0).astype(jnp.bfloat16)  41.5 us
    convert_element_type x2, other arithmetic, slopes_of(): field = padded.astype(jnp.float32)  20.3 us
  transfers between devices with their start and end apart: 3, of which 1 were waited for; matrix products, arithmetic and copies ran while one was open for 77% of the time, Pallas kernels for 0%

commit v1 on v0

v1 whole, which is shorter than its diff:
```python
import jax
import jax.numpy as jnp
from jax import lax
from jax.experimental import pallas as pl
from jax.experimental.pallas import tpu as pltpu
from jax.sharding import PartitionSpec as P

MESH = pl.DeviceIdType.MESH
F32 = jnp.float32
BF16 = jnp.bfloat16
E = 2048
EL = 128
QUADS = 32768
QK = 2048
ROWS = 80
WIN = 1280
NC = 768


def kernel(pot, quad, res, weight, out,
           uf, lo, hi, hf, sb, S, Tb, gs, gr,
           halo_s, halo_r, fs, fr, ws, wr, z_s, z_r, p2_s, p2_r, p3_s, p3_r, g_s, g_r):
    e = lax.axis_index("elec")
    s = lax.axis_index("space")
    zh, x, c = e // 8, (e // 2) % 4, e % 2
    zl, y = s // 4, s % 4
    z = zh * 4 + zl
    mi = zh * 4 + x

    def elec_peer(k):
        return (lax.rem(e + k, 16), s)

    def space_peer(d):
        return (e, lax.rem(s + d + 16, 16))

    def z_peer(d):
        t = lax.rem(z + d, 8)
        return ((t // 4) * 8 + x * 2 + c, lax.rem(t, 4) * 4 + y)

    def x_peer(d):
        return (zh * 8 + lax.rem(x + d, 4) * 2 + c, s)

    def y_peer(d):
        return (e, zl * 4 + lax.rem(y + d, 4))

    other_core = (zh * 8 + x * 2 + (1 - c), s)

    def remote(src, dst, ss, rs, device):
        return pltpu.make_async_remote_copy(
            src_ref=src, dst_ref=dst, send_sem=ss, recv_sem=rs, device_id=device, device_id_type=MESH)

    barrier = pltpu.get_barrier_semaphore()
    peers = ([elec_peer(k) for k in range(1, 16)] + [space_peer(1), space_peer(-1)]
             + [z_peer(d) for d in (1, 2, 3, 5, 6, 7)] + [y_peer(d) for d in (1, 2, 3)])
    for peer in peers:
        pl.semaphore_signal(barrier, inc=1, device_id=peer, device_id_type=MESH)

    uf[...] = pot[...].astype(F32).reshape(EL * 16, 128)
    pl.semaphore_wait(barrier, len(peers))

    up = remote(pot.at[:, 1], lo, halo_s.at[0], halo_r.at[0], space_peer(1))
    down = remote(pot.at[:, 0], hi, halo_s.at[1], halo_r.at[1], space_peer(-1))
    up.start()
    down.start()

    lane = lax.broadcasted_iota(jnp.int32, (EL, 128), 1)

    def target(j):
        dz = jnp.where(j < 4, 1, 0)
        dx = jnp.where(j < 4, j, j - 3)
        return lax.rem(zh + dz, 2), lax.rem(x + dx, 4)

    def source(j):
        dz = jnp.where(j < 4, 1, 0)
        dx = jnp.where(j < 4, j, j - 3)
        return (lax.rem(zh + dz, 2) * 8 + lax.rem(x + 4 - lax.rem(dx, 4), 4) * 2 + c) * EL

    def field_copy(j, part):
        tz, tx = target(j)
        m = tz * 4 + tx
        cols = pl.ds(0, 512) if part == 0 else pl.ds(512, 256)
        return remote(sb.at[m, :, cols], S.at[pl.ds(pl.multiple_of(e * EL, EL), EL), cols],
                      fs.at[part, j], fr.at[part, j], (tz * 8 + tx * 2 + c, s))

    def column(ref, start, stride):
        return ref[pl.ds(start, EL, stride=stride), :]

    def zy_step(j, carry):
        tz, tx = target(j)
        m = tz * 4 + tx
        for p in range(2):
            u = column(uf, p * 8 + m, 16)
            before = jnp.where(m > 0, column(uf, p * 8 + jnp.maximum(m - 1, 0), 16), 0.0)
            after = jnp.where(m < 7, column(uf, p * 8 + jnp.minimum(m + 1, 7), 16), 0.0)
            left = jnp.where(lane > 0, pltpu.roll(u, 1, axis=1), 0.0)
            right = jnp.where(lane < 127, pltpu.roll(u, 127, axis=1), 0.0)
            sb[m, :, p * 128:p * 128 + 128] = (0.5 * (right - left)).astype(BF16)
            sb[m, :, 256 + p * 128:256 + p * 128 + 128] = (0.5 * (after - before)).astype(BF16)

        @pl.when(j < 7)
        def _():
            field_copy(j, 0).start()

        return carry

    lax.fori_loop(0, 8, zy_step, 0)

    rb = jnp.where(z < 4, y * 4 + x, x * 4 + y)
    col0 = c * 1024 + z * 128
    row0 = (c * 4 + z // 2) * 256 + rb * ROWS
    row_ids = ((lax.broadcasted_iota(jnp.int32, (ROWS, QK), 0) + row0) & (E - 1)).astype(jnp.int16)
    col_ids = (lax.broadcasted_iota(jnp.int32, (EL, QK), 0) + col0).astype(jnp.int16)
    one = jnp.ones((16, QK), BF16)
    zero = jnp.zeros((16, QK), BF16)

    def hot(u, v, ids, plus, minus):
        return jnp.concatenate(
            [jnp.where(u == ids[k:k + 16], plus, jnp.where(v == ids[k:k + 16], minus, zero))
             for k in range(0, ids.shape[0], 16)], axis=0)

    def nt(a, b):
        return lax.dot_general(a, b, (((1,), (1,)), ((), ())), preferred_element_type=F32)

    def quad_step(i, acc):
        q = pl.ds(pl.multiple_of(i * QK, QK), QK)
        a, b, m, n = (quad[k:k + 1, q] for k in range(4))
        r = jnp.where((a == b) | (m == n), 0.0, res[0:1, q])
        a, b, m, n = (jnp.broadcast_to(v, (16, QK)).astype(jnp.int16) for v in (a, b, m, n))
        r = jnp.broadcast_to(r, (16, QK)).astype(BF16)
        acc = acc + nt(hot(a, b, row_ids, one, -one), hot(m, n, col_ids, r, -r))
        return acc + nt(hot(m, n, row_ids, one, -one), hot(a, b, col_ids, r, -r))

    block = lax.fori_loop(0, QUADS // QK, quad_step, jnp.zeros((ROWS, EL), F32))
    offset = lax.broadcasted_iota(jnp.int32, (ROWS, EL), 0) + rb * ROWS
    block = jnp.where((offset < 256) | (offset >= 1024), 0.5 * block, block)
    own = pl.ds(pl.multiple_of(rb * ROWS, 16), ROWS)
    Tb[z, own, :] = block.astype(BF16)

    def z_copy(d):
        return remote(Tb.at[z, own], Tb.at[z, own], z_s.at[d - 1], z_r.at[d - 1], z_peer(d))

    for d in range(1, 8):
        z_copy(d).start()

    up.wait_recv()
    down.wait_recv()
    hf[0:EL * 8, :] = jnp.where(s > 0, lo[...].astype(F32).reshape(EL * 8, 128), 0.0)
    hf[EL * 8:, :] = jnp.where(s < 15, hi[...].astype(F32).reshape(EL * 8, 128), 0.0)

    def x_step(j, carry):
        tz, tx = target(j)
        m = tz * 4 + tx
        u0, u1 = column(uf, m, 16), column(uf, 8 + m, 16)
        low, high = column(hf, m, 8), column(hf, EL * 8 + m, 8)
        sb[m, :, 512:640] = (0.5 * (u1 - low)).astype(BF16)
        sb[m, :, 640:768] = (0.5 * (high - u0)).astype(BF16)

        @pl.when(j < 7)
        def _():
            field_copy(j, 1).start()

        return carry

    lax.fori_loop(0, 8, x_step, 0)

    def forward(j):
        rows = pl.ds(pl.multiple_of(source(j), EL), EL)
        return remote(S.at[rows], S.at[rows], ws.at[j], wr.at[j], other_core)

    S[pl.ds(pl.multiple_of(e * EL, EL), EL), :] = sb[mi]
    forward(7).start()

    slab_a = pl.ds(pl.multiple_of((y * 4 + x) * ROWS, 16), ROWS)
    slab_b = pl.ds(pl.multiple_of((x * 4 + y) * ROWS, 16), ROWS)
    wide_a = pl.ds(pl.multiple_of(y * 4 * ROWS, 16), 4 * ROWS)
    wide_b = pl.ds(pl.multiple_of(x * 4 * ROWS, 16), 4 * ROWS)

    def slab_copies(d):
        a, b = Tb.at[0:4, slab_a], Tb.at[4:8, slab_b]
        return (remote(a, a, p2_s.at[0, d - 1], p2_r.at[0, d - 1], x_peer(d)),
                remote(b, b, p2_s.at[1, d - 1], p2_r.at[1, d - 1], y_peer(d)))

    def wide_copies(d):
        a, b = Tb.at[0:4, wide_a], Tb.at[4:8, wide_b]
        return (remote(a, a, p3_s.at[0, d - 1], p3_r.at[0, d - 1], y_peer(d)),
                remote(b, b, p3_s.at[1, d - 1], p3_r.at[1, d - 1], x_peer(d)))

    for d in range(1, 8):
        z_copy(d).wait_recv()
    for d in range(1, 4):
        for copy in slab_copies(d):
            copy.start()

    def forward_step(j, carry):
        field_copy(j, 0).wait_recv()
        field_copy(j, 1).wait_recv()
        forward(j).start()
        return carry

    lax.fori_loop(4, 7, forward_step, 0)
    for d in range(1, 4):
        for copy in slab_copies(d):
            copy.wait_recv()
    for d in range(1, 4):
        for copy in wide_copies(d):
            copy.start()
    lax.fori_loop(0, 4, forward_step, 0)
    for d in range(1, 4):
        for copy in wide_copies(d):
            copy.wait_recv()

    def forwarded(j, carry):
        forward(j).wait_recv()
        return carry

    lax.fori_loop(0, 8, forwarded, 0)

    def block_step(jj, acc):
        lhs = jnp.concatenate([Tb[2 * jj], Tb[2 * jj + 1]], axis=1)
        first = c * 4 + jj
        sums = []
        for n in range(3):
            cols = slice(n * 256, n * 256 + 256)
            rhs = S[pl.ds(pl.multiple_of(first * 256, 256), 256), cols]
            image = jnp.dot(lhs, rhs, preferred_element_type=F32)
            total = jnp.zeros((8, 256), F32)
            for d in range(5):
                rows = pl.ds(pl.multiple_of(lax.rem(first + d, 8) * 256, 256), 256)
                prod = image[d * 256:d * 256 + 256] * S[rows, cols].astype(F32)
                total = total + jnp.sum(prod.reshape(32, 8, 256), axis=0)
            sums.append(total)
        return acc + (sums[0] + sums[1] + sums[2])

    total = lax.fori_loop(0, 4, block_step, jnp.zeros((8, 256), F32))
    total = jnp.sum(total, axis=0, keepdims=True)
    gs[...] = jnp.zeros((8, 128), F32)
    gs[0:1, :] = total[:, 0:128]
    gs[1:2, :] = total[:, 128:256]

    def share(k):
        return remote(gs, gr.at[e], g_s.at[k - 1], g_r.at[k - 1], elec_peer(k))

    for k in range(1, 16):
        share(k).start()
    gr[e] = gs[...]
    for k in range(1, 16):
        share(k).wait_recv()
    for m in range(8):
        both = gr[2 * m] + gr[2 * m + 1]
        for p in range(2):
            out[p, m:m + 1, :] = both[p:p + 1, :] * weight[p, m:m + 1, :]

    up.wait_send()
    down.wait_send()

    def sent(j, carry):
        field_copy(j, 0).wait_send()
        field_copy(j, 1).wait_send()
        return carry

    lax.fori_loop(0, 7, sent, 0)

    def passed(j, carry):
        forward(j).wait_send()
        return carry

    lax.fori_loop(0, 8, passed, 0)
    for d in range(1, 8):
        z_copy(d).wait_send()
    for d in range(1, 4):
        for copy in slab_copies(d) + wide_copies(d):
            copy.wait_send()
    for k in range(1, 16):
        share(k).wait_send()


def local(potentials, quadrupoles, residuals, cell_weight):
    dma = pltpu.SemaphoreType.DMA
    return pl.pallas_call(
        kernel,
        name="misfit_gradient",
        out_shape=jax.ShapeDtypeStruct(cell_weight.shape, F32),
        in_specs=[pl.BlockSpec(memory_space=pltpu.VMEM)] * 4,
        out_specs=pl.BlockSpec(memory_space=pltpu.VMEM),
        scratch_shapes=[
            pltpu.VMEM((EL * 16, 128), F32),
            pltpu.VMEM((EL, 8, 128), BF16),
            pltpu.VMEM((EL, 8, 128), BF16),
            pltpu.VMEM((EL * 16, 128), F32),
            pltpu.VMEM((8, EL, NC), BF16),
            pltpu.VMEM((E, NC), BF16),
            pltpu.VMEM((8, WIN, 128), BF16),
            pltpu.VMEM((8, 128), F32),
            pltpu.VMEM((16, 8, 128), F32),
            dma((2,)), dma((2,)),
            dma((2, 7)), dma((2, 7)),
            dma((8,)), dma((8,)),
            dma((7,)), dma((7,)),
            dma((2, 3)), dma((2, 3)),
            dma((2, 3)), dma((2, 3)),
            dma((15,)), dma((15,)),
        ],
        compiler_params=pltpu.CompilerParams(
            collective_id=0, has_side_effects=True, vmem_limit_bytes=56 << 20),
    )(potentials, quadrupoles, residuals.reshape(1, QUADS), cell_weight)


def solution(mesh):
    placed = (P("elec", "space", None, None), P(), P(), P("space", None, None))
    return jax.shard_map(
        local, mesh=mesh, in_specs=placed, out_specs=P("space", None, None), check_vma=False
    )
```

time: 908 us -> 89.4 us (0.10)
  the two profiles are of different devices: /device:TPU:32 before, /device:TPU:1 now
where the time goes in v1:
time: 89.4 us; the launch traced here: 89.3 us
  Pallas kernels  88 us (98%)
  local copies, waits for them, and re-layouts  1.3 us (1%)
    pallas_call x1, Pallas kernels, local(): pl.pallas_call(kernel, name='misfit_gradient', out_shape=jax.ShapeDtypeSt...  88 us

profile of v1, /device:TPU:1, one launch (start us, length us, event | category | flops | bytes accessed | tf_op | source)
XLA Modules:
  0.0 89.3 jit_solution(7233589675100376905)
XLA Ops:
  0.0 88.0 %misfit_gradient.1 = f32[2,8,128]{2,1,0:T(8,128)} custom-call(bf16[128,2,8,128]{3,2,1,0:T(8,128)(2,1)} %pot.1, s32[4,32768]{1,0:T(4,128)} %quad.1, f32[1,32768]{1,0:T(1,128)} %bitcast.1, f32[2,8,128]{2,1,0:T(8,128)} %weight.1), custom_call_target="tpu_custom_call" | custom-call | tf_op jit(solution)/shard_map/misfit_gradient/pallas_call | solution.py:279
  88.0 1.3 %copy.6 = f32[2,8,128]{2,1,0:T(8,128)} copy(f32[2,8,128]{2,1,0:T(8,128)} %misfit_gradient.1) | data formatting | bytes 16384

commit v2 on v1

v2 whole, which is shorter than its diff:
```python
import jax
import jax.numpy as jnp
from jax import lax
from jax.experimental import pallas as pl
from jax.experimental.pallas import tpu as pltpu
from jax.sharding import PartitionSpec as P

MESH = pl.DeviceIdType.MESH
F32 = jnp.float32
BF16 = jnp.bfloat16
E = 2048
EL = 128
QUADS = 32768
QK = 2048
ROWS = 80
WIN = 1280
NA = 6
PIECES = ((0, 0, 128), (1, 0, 64), (1, 64, 64))
NC = 768


def kernel(pot, quad, res, weight, out,
           uf, W, sr, H, sb, S, Tb, gs, gr,
           r_s, r_r, halo_s, halo_r, fs, fr, ws, wr, z_s, z_r, p2_s, p2_r, p3_s, p3_r, p4_s, p4_r, g_s, g_r):
    e = lax.axis_index("elec")
    s = lax.axis_index("space")
    zh, x, c = e // 8, (e // 2) % 4, e % 2
    zl, y = s // 4, s % 4
    z = zh * 4 + zl

    def elec_peer(k):
        return (lax.rem(e + k, 16), s)

    def space_peer(d):
        return (e, lax.rem(s + d + 16, 16))

    def z_peer(d):
        t = lax.rem(z + d, 8)
        return ((t // 4) * 8 + x * 2 + c, lax.rem(t, 4) * 4 + y)

    def x_peer(d):
        return (zh * 8 + lax.rem(x + d, 4) * 2 + c, s)

    def y_peer(d):
        return (e, zl * 4 + lax.rem(y + d, 4))

    other_core = (zh * 8 + x * 2 + (1 - c), s)
    partner = lax.rem(e + 8, 16)

    def remote(src, dst, ss, rs, device):
        return pltpu.make_async_remote_copy(
            src_ref=src, dst_ref=dst, send_sem=ss, recv_sem=rs, device_id=device, device_id_type=MESH)

    barrier = pltpu.get_barrier_semaphore()
    peers = ([elec_peer(k) for k in range(1, 16)] + [space_peer(1), space_peer(-1)]
             + [z_peer(d) for d in (1, 2, 3, 5, 6, 7)] + [y_peer(d) for d in (1, 2, 3)])
    for peer in peers:
        pl.semaphore_signal(barrier, inc=1, device_id=peer, device_id_type=MESH)

    uf[...] = pot[...].astype(F32).reshape(EL * 16, 128)

    def half_step(i, carry):
        for p in range(2):
            mine = zh * 4 + i - 1
            u = uf[pl.ds(p * 8 + jnp.clip(mine, 0, 7), EL, stride=16), :]
            W[0, i, p] = jnp.where((mine >= 0) & (mine < 8), u, 0.0).astype(BF16)
            theirs = (1 - zh) * 4 + i - 1
            sr[i, p] = uf[pl.ds(p * 8 + jnp.clip(theirs, 0, 7), EL, stride=16), :].astype(BF16)
        return carry

    lax.fori_loop(0, 6, half_step, 0)
    W[1, 5 * zh] = jnp.zeros((2, EL, 128), BF16)

    @pl.when(s == 0)
    def _():
        H[:, 0] = jnp.zeros((2, 4, EL, 128), BF16)

    @pl.when(s == 15)
    def _():
        H[:, 1] = jnp.zeros((2, 4, EL, 128), BF16)

    rb = jnp.where(z < NA, y * 4 + x, x * 4 + y)
    col0 = c * 1024 + z * 128
    row0 = (c * 4 + z // 2) * 256 + rb * ROWS
    row_ids = ((lax.broadcasted_iota(jnp.int32, (ROWS, QK), 0) + row0) & (E - 1)).astype(jnp.int16)
    col_ids = (lax.broadcasted_iota(jnp.int32, (EL, QK), 0) + col0).astype(jnp.int16)
    one = jnp.ones((16, QK), BF16)
    zero = jnp.zeros((16, QK), BF16)

    def hot(u, v, ids, plus, minus):
        return jnp.concatenate(
            [jnp.where(u == ids[k:k + 16], plus, jnp.where(v == ids[k:k + 16], minus, zero))
             for k in range(0, ids.shape[0], 16)], axis=0)

    def nt(a, b):
        return lax.dot_general(a, b, (((1,), (1,)), ((), ())), preferred_element_type=F32)

    def quad_step(i, acc):
        q = pl.ds(pl.multiple_of(i * QK, QK), QK)
        a, b, m, n = (quad[k:k + 1, q] for k in range(4))
        r = jnp.where((a == b) | (m == n), 0.0, res[0:1, q])
        a, b, m, n = (jnp.broadcast_to(v, (16, QK)).astype(jnp.int16) for v in (a, b, m, n))
        r = jnp.broadcast_to(r, (16, QK)).astype(BF16)
        acc = acc + nt(hot(a, b, row_ids, one, -one), hot(m, n, col_ids, r, -r))
        return acc + nt(hot(m, n, row_ids, one, -one), hot(a, b, col_ids, r, -r))

    block = lax.fori_loop(0, QUADS // QK, quad_step, jnp.zeros((ROWS, EL), F32))
    offset = lax.broadcasted_iota(jnp.int32, (ROWS, EL), 0) + rb * ROWS
    block = jnp.where((offset < 256) | (offset >= 1024), 0.5 * block, block)
    own = pl.ds(pl.multiple_of(rb * ROWS, 16), ROWS)
    Tb[z, own, :] = block.astype(BF16)

    pl.semaphore_wait(barrier, len(peers))

    raw = pl.ds(zh, 5)

    def raw_copy(i):
        _, lo, n = PIECES[i]
        return remote(sr.at[raw, :, lo:lo + n], W.at[1, raw, :, lo:lo + n], r_s.at[i - 1], r_r.at[i - 1], (partner, s))

    def halo_copies(i):
        g, lo, n = PIECES[i]
        return (remote(W.at[g, 1:5, 1, lo:lo + n], H.at[g, 0, :, lo:lo + n],
                       halo_s.at[i, 0], halo_r.at[i, 0], space_peer(1)),
                remote(W.at[g, 1:5, 0, lo:lo + n], H.at[g, 1, :, lo:lo + n],
                       halo_s.at[i, 1], halo_r.at[i, 1], space_peer(-1)))

    def start_halo(i):
        up, down = halo_copies(i)

        @pl.when(s < 15)
        def _():
            up.start()

        @pl.when(s > 0)
        def _():
            down.start()

    def halo_arrived(i):
        up, down = halo_copies(i)

        @pl.when(s > 0)
        def _():
            up.wait_recv()

        @pl.when(s < 15)
        def _():
            down.wait_recv()

    def halo_sent(i):
        up, down = halo_copies(i)

        @pl.when(s < 15)
        def _():
            up.wait_send()

        @pl.when(s > 0)
        def _():
            down.wait_send()

    def z_copy(d):
        return remote(Tb.at[z, own], Tb.at[z, own], z_s.at[d - 1], z_r.at[d - 1], z_peer(d))

    start_halo(0)
    for d in range(1, 8):
        z_copy(d).start()
    def electrodes(i, origin):
        _, lo, n = PIECES[i]
        return pl.ds(pl.multiple_of(origin * EL + lo, 64), n)

    def group(i):
        return e if PIECES[i][0] == 0 else partner

    def field_copy(i, d, part):
        g, lo, n = PIECES[i]
        tx = lax.rem(x + d, 4)
        cols = pl.ds(0, 512) if part == 0 else pl.ds(512, 256)
        return remote(sb.at[g, tx, lo:lo + n, cols], S.at[electrodes(i, group(i)), cols],
                      fs.at[i, part, d - 1], fr.at[i, part, d - 1], x_peer(d))

    def zy_slopes(i):
        g, lo, n = PIECES[i]
        rows = slice(lo, lo + n)
        lane = lax.broadcasted_iota(jnp.int32, (n, 128), 1)

        def step(j, carry):
            t = lax.rem(x + j, 4)
            for p in range(2):
                u = W[g, t + 1, p, rows].astype(F32)
                before, after = W[g, t, p, rows].astype(F32), W[g, t + 2, p, rows].astype(F32)
                left = jnp.where(lane > 0, pltpu.roll(u, 1, axis=1), 0.0)
                right = jnp.where(lane < 127, pltpu.roll(u, 127, axis=1), 0.0)
                sb[g, t, rows, p * 128:p * 128 + 128] = (0.5 * (right - left)).astype(BF16)
                sb[g, t, rows, 256 + p * 128:256 + p * 128 + 128] = (0.5 * (after - before)).astype(BF16)

            @pl.when(j < 4)
            def _():
                field_copy(i, j, 0).start()

            return carry

        lax.fori_loop(1, 5, step, 0)

    def x_slopes(i):
        g, lo, n = PIECES[i]
        rows = slice(lo, lo + n)

        def step(j, carry):
            t = lax.rem(x + j, 4)
            u0, u1 = W[g, t + 1, 0, rows].astype(F32), W[g, t + 1, 1, rows].astype(F32)
            low, high = H[g, 0, t, rows].astype(F32), H[g, 1, t, rows].astype(F32)
            sb[g, t, rows, 512:640] = (0.5 * (u1 - low)).astype(BF16)
            sb[g, t, rows, 640:768] = (0.5 * (high - u0)).astype(BF16)

            @pl.when(j < 4)
            def _():
                field_copy(i, j, 1).start()

            return carry

        lax.fori_loop(1, 5, step, 0)
        S[electrodes(i, group(i)), :] = sb[g, x, rows]

    def forward(i, d):
        origin = (zh if PIECES[i][0] == 0 else 1 - zh) * 8 + lax.rem(x + 4 - d, 4) * 2 + c
        rows = electrodes(i, origin)
        return remote(S.at[rows], S.at[rows], ws.at[i, d], wr.at[i, d], other_core)

    def slab(a, b):
        return pl.ds(pl.multiple_of((a * 4 + b) * ROWS, 16), ROWS)

    wide_b = pl.ds(pl.multiple_of(x * 4 * ROWS, 16), 4 * ROWS)

    def slab_copies(d):
        a, b = Tb.at[0:NA, slab(y, x)], Tb.at[NA:8, slab(x, y)]
        return (remote(a, a, p2_s.at[0, d - 1], p2_r.at[0, d - 1], x_peer(d)),
                remote(b, b, p2_s.at[1, d - 1], p2_r.at[1, d - 1], y_peer(d)))

    def wide_copy(d, dy):
        a = Tb.at[0:NA, slab(y, lax.rem(x + 4 - d, 4))]
        return remote(a, a, p3_s.at[d, dy - 1], p3_r.at[d, dy - 1], y_peer(dy))

    def wide_copy_b(d):
        b = Tb.at[NA:8, wide_b]
        return remote(b, b, p4_s.at[d - 1], p4_r.at[d - 1], x_peer(d))

    def pass_on(i, d):
        field_copy(i, d, 0).wait_recv()
        field_copy(i, d, 1).wait_recv()
        forward(i, d).start()

    def start_all(copies):
        for copy in copies:
            copy.start()

    def arrived(copies):
        for copy in copies:
            copy.wait_recv()

    arrived(z_copy(d) for d in range(1, 8))
    raw_copy(1).start()
    raw_copy(2).start()
    for d in range(1, 4):
        start_all(slab_copies(d))
    start_all(wide_copy(0, dy) for dy in (1, 3, 2))
    zy_slopes(0)
    halo_arrived(0)
    x_slopes(0)
    forward(0, 0).start()
    for d in (1, 3, 2):
        arrived(slab_copies(d))
        start_all(wide_copy(d, dy) for dy in (1, 3, 2))
    start_all(wide_copy_b(d) for d in (1, 3, 2))
    raw_copy(1).wait_recv()
    start_halo(1)
    zy_slopes(1)
    halo_arrived(1)
    x_slopes(1)
    forward(1, 0).start()
    raw_copy(2).wait_recv()
    start_halo(2)
    zy_slopes(2)
    for d in (1, 3, 2):
        pass_on(0, d)
    halo_arrived(2)
    x_slopes(2)
    forward(2, 0).start()
    for i in (1, 2):
        for d in (1, 3, 2):
            pass_on(i, d)
    for i in range(3):
        arrived(forward(i, d) for d in range(4))

    def product(jj, k, acc):
        rows = pl.ds(pl.multiple_of(k * 4 * ROWS, 16), 4 * ROWS)
        lhs = jnp.concatenate([Tb[2 * jj, rows], Tb[2 * jj + 1, rows]], axis=1)
        first = (c * 4 + jj) * 256
        for n in range(3):
            cols = slice(n * 256, n * 256 + 256)
            image = jnp.dot(lhs, S[pl.ds(pl.multiple_of(first, 256), 256), cols], preferred_element_type=F32)
            for b in range(5):
                own_rows = pl.ds(pl.multiple_of((first + k * 4 * ROWS + b * 64) & (E - 1), 64), 64)
                prod = image[b * 64:b * 64 + 64] * S[own_rows, cols].astype(F32)
                acc = acc + jnp.sum(prod.reshape(8, 8, 256), axis=0)
        return acc

    total = jnp.zeros((8, 256), F32)
    for d in (0, 1, 3, 2):
        if d > 0:
            arrived(wide_copy(o, d) for o in range(4))
        total = lax.fori_loop(0, NA // 2, lambda jj, acc: product(jj, lax.rem(y + 4 - d, 4), acc), total)
    for d in (0, 1, 3, 2) if NA < 8 else ():
        if d > 0:
            wide_copy_b(d).wait_recv()
        total = lax.fori_loop(NA // 2, 4, lambda jj, acc: product(jj, lax.rem(x + 4 - d, 4), acc), total)
    total = jnp.sum(total, axis=0, keepdims=True)
    gs[...] = jnp.zeros((8, 128), F32)
    gs[0:1, :] = total[:, 0:128]
    gs[1:2, :] = total[:, 128:256]

    def share(k):
        return remote(gs, gr.at[e], g_s.at[k - 1], g_r.at[k - 1], elec_peer(k))

    for k in range(1, 16):
        share(k).start()
    gr[e] = gs[...]
    for k in range(1, 16):
        share(k).wait_recv()
    for m in range(8):
        both = gr[2 * m] + gr[2 * m + 1]
        for p in range(2):
            out[p, m:m + 1, :] = both[p:p + 1, :] * weight[p, m:m + 1, :]


    sent = [raw_copy(1), raw_copy(2)]
    for i in range(3):
        halo_sent(i)
        sent += [field_copy(i, d, part) for d in range(1, 4) for part in range(2)]
        sent += [forward(i, d) for d in range(4)]
    sent += [z_copy(d) for d in range(1, 8)]
    for d in range(1, 4):
        sent += slab_copies(d)
        sent += [wide_copy(o, d) for o in range(4)]
        sent += [wide_copy_b(d)]
    sent += [share(k) for k in range(1, 16)]
    for copy in sent:
        copy.wait_send()


def local(potentials, quadrupoles, residuals, cell_weight):
    dma = pltpu.SemaphoreType.DMA
    return pl.pallas_call(
        kernel,
        name="misfit_gradient",
        out_shape=jax.ShapeDtypeStruct(cell_weight.shape, F32),
        in_specs=[pl.BlockSpec(memory_space=pltpu.VMEM)] * 4,
        out_specs=pl.BlockSpec(memory_space=pltpu.VMEM),
        scratch_shapes=[
            pltpu.VMEM((EL * 16, 128), F32),
            pltpu.VMEM((2, 6, 2, EL, 128), BF16),
            pltpu.VMEM((6, 2, EL, 128), BF16),
            pltpu.VMEM((2, 2, 4, EL, 128), BF16),
            pltpu.VMEM((2, 4, EL, NC), BF16),
            pltpu.VMEM((E, NC), BF16),
            pltpu.VMEM((8, WIN, 128), BF16),
            pltpu.VMEM((8, 128), F32),
            pltpu.VMEM((16, 8, 128), F32),
            dma((2,)), dma((2,)),
            dma((3, 2)), dma((3, 2)),
            dma((3, 2, 3)), dma((3, 2, 3)),
            dma((3, 4)), dma((3, 4)),
            dma((7,)), dma((7,)),
            dma((2, 3)), dma((2, 3)),
            dma((4, 3)), dma((4, 3)),
            dma((3,)), dma((3,)),
            dma((15,)), dma((15,)),
        ],
        compiler_params=pltpu.CompilerParams(
            collective_id=0, has_side_effects=True, vmem_limit_bytes=56 << 20),
    )(potentials, quadrupoles, residuals.reshape(1, QUADS), cell_weight)


def solution(mesh):
    placed = (P("elec", "space", None, None), P(), P(), P("space", None, None))
    return jax.shard_map(
        local, mesh=mesh, in_specs=placed, out_specs=P("space", None, None), check_vma=False
    )
```

time: 89.4 us -> 72.5 us (0.81)
  the two profiles are of different devices: /device:TPU:1 before, /device:TPU:32 now
where the time goes in v2:
time: 72.5 us; the launch traced here: 71.1 us
  Pallas kernels  69.8 us (96%)
  local copies, waits for them, and re-layouts  1.3 us (2%)
    pallas_call x1, Pallas kernels, local(): pl.pallas_call(kernel, name='misfit_gradient', out_shape=jax.ShapeDtypeSt...  69.8 us

profile of v2, /device:TPU:32, one launch (start us, length us, event | category | flops | bytes accessed | tf_op | source)
XLA Modules:
  0.0 71.1 jit_solution(1825288822882219103)
XLA Ops:
  0.0 69.8 %misfit_gradient.1 = f32[2,8,128]{2,1,0:T(8,128)} custom-call(bf16[128,2,8,128]{3,2,1,0:T(8,128)(2,1)} %pot.1, s32[4,32768]{1,0:T(4,128)} %quad.1, f32[1,32768]{1,0:T(1,128)} %bitcast.1, f32[2,8,128]{2,1,0:T(8,128)} %weight.1), custom_call_target="tpu_custom_call" | custom-call | tf_op jit(solution)/shard_map/misfit_gradient/pallas_call | solution.py:352
  69.8 1.3 %copy.6 = f32[2,8,128]{2,1,0:T(8,128)} copy(f32[2,8,128]{2,1,0:T(8,128)} %misfit_gradient.1) | data formatting | bytes 16384

commit v3 on v2

v3 whole, which is shorter than its diff:
```python
import jax
import jax.numpy as jnp
from jax import lax
from jax.experimental import pallas as pl
from jax.experimental.pallas import tpu as pltpu
from jax.sharding import PartitionSpec as P

MESH = pl.DeviceIdType.MESH
F32 = jnp.float32
BF16 = jnp.bfloat16
E = 2048
EL = 128
QUADS = 32768
QK = 4096
ROWS = 80
WIN = 1280
PIECES = ((0, 0, 128), (1, 0, 64), (1, 64, 64))
NC = 768


def kernel(pot, quad, res, weight, out,
           uf, W, sr, H, sb, S, Tb, gs, gx, gt, gr,
           r_s, r_r, halo_s, halo_r, fs, fr, ws, wr, z_s, z_r, p2_s, p2_r, p3_s, p3_r, p4_s, p4_r, c_s, c_r, g_s, g_r):
    e = lax.axis_index("elec")
    s = lax.axis_index("space")
    zh, x, c = e // 8, (e // 2) % 4, e % 2
    zl, y = s // 4, s % 4
    z = zh * 4 + zl
    mi = zh * 4 + x

    def chip_peer(k):
        return (lax.rem(mi + k, 8) * 2 + c, s)

    def space_peer(d):
        return (e, lax.rem(s + d + 16, 16))

    def z_peer(d):
        t = lax.rem(z + d, 8)
        return ((t // 4) * 8 + x * 2 + c, lax.rem(t, 4) * 4 + y)

    def x_peer(d):
        return (zh * 8 + lax.rem(x + d, 4) * 2 + c, s)

    def y_peer(d):
        return (e, zl * 4 + lax.rem(y + d, 4))

    other_core = (zh * 8 + x * 2 + (1 - c), s)
    partner = lax.rem(e + 8, 16)

    def remote(src, dst, ss, rs, device):
        return pltpu.make_async_remote_copy(
            src_ref=src, dst_ref=dst, send_sem=ss, recv_sem=rs, device_id=device, device_id_type=MESH)

    barrier = pltpu.get_barrier_semaphore()
    peers = ([chip_peer(k) for k in range(1, 8)] + [other_core, space_peer(1), space_peer(-1)]
             + [z_peer(d) for d in (1, 2, 3, 5, 6, 7)] + [y_peer(d) for d in (1, 2, 3)])
    for peer in peers:
        pl.semaphore_signal(barrier, inc=1, device_id=peer, device_id_type=MESH)

    rb = y * 4 + x
    col0 = c * 1024 + z * 128
    row0 = (c * 4 + z // 2) * 256 + rb * ROWS
    row_ids = ((lax.broadcasted_iota(jnp.int32, (ROWS, QK), 0) + row0) & (E - 1)).astype(jnp.int16)
    col_ids = (lax.broadcasted_iota(jnp.int32, (EL, QK), 0) + col0).astype(jnp.int16)
    one = jnp.ones((16, QK), BF16)
    zero = jnp.zeros((16, QK), BF16)

    def hot(u, v, ids, plus, minus):
        return jnp.concatenate(
            [jnp.where(u == ids[k:k + 16], plus, jnp.where(v == ids[k:k + 16], minus, zero))
             for k in range(0, ids.shape[0], 16)], axis=0)

    def nt(a, b):
        return lax.dot_general(a, b, (((1,), (1,)), ((), ())), preferred_element_type=F32)

    def quad_step(i, acc):
        q = pl.ds(pl.multiple_of(i * QK, QK), QK)
        a, b, m, n = (quad[k:k + 1, q] for k in range(4))
        r = jnp.where((a == b) | (m == n), 0.0, res[0:1, q])
        a, b, m, n = (jnp.broadcast_to(v, (16, QK)).astype(jnp.int16) for v in (a, b, m, n))
        r = jnp.broadcast_to(r, (16, QK)).astype(BF16)
        acc = acc + nt(hot(a, b, row_ids, one, -one), hot(m, n, col_ids, r, -r))
        return acc + nt(hot(m, n, row_ids, one, -one), hot(a, b, col_ids, r, -r))

    block = lax.fori_loop(0, QUADS // QK, quad_step, jnp.zeros((ROWS, EL), F32))
    offset = lax.broadcasted_iota(jnp.int32, (ROWS, EL), 0) + rb * ROWS
    block = jnp.where((offset < 256) | (offset >= 1024), 0.5 * block, block)
    own = pl.ds(pl.multiple_of(rb * ROWS, 16), ROWS)
    Tb[z, own, :] = block.astype(BF16)

    pl.semaphore_wait(barrier, len(peers))

    raw = pl.ds(zh, 5)

    def raw_copy(i):
        _, lo, n = PIECES[i]
        return remote(sr.at[raw, :, lo:lo + n], W.at[1, raw, :, lo:lo + n], r_s.at[i - 1], r_r.at[i - 1], (partner, s))

    def halo_copies(i):
        g, lo, n = PIECES[i]
        return (remote(W.at[g, 1:5, 1, lo:lo + n], H.at[g, 0, :, lo:lo + n],
                       halo_s.at[i, 0], halo_r.at[i, 0], space_peer(1)),
                remote(W.at[g, 1:5, 0, lo:lo + n], H.at[g, 1, :, lo:lo + n],
                       halo_s.at[i, 1], halo_r.at[i, 1], space_peer(-1)))

    def start_halo(i):
        up, down = halo_copies(i)

        @pl.when(s < 15)
        def _():
            up.start()

        @pl.when(s > 0)
        def _():
            down.start()

    def halo_arrived(i):
        up, down = halo_copies(i)

        @pl.when(s > 0)
        def _():
            up.wait_recv()

        @pl.when(s < 15)
        def _():
            down.wait_recv()

    def halo_sent(i):
        up, down = halo_copies(i)

        @pl.when(s < 15)
        def _():
            up.wait_send()

        @pl.when(s > 0)
        def _():
            down.wait_send()

    def z_copy(d):
        return remote(Tb.at[z, own], Tb.at[z, own], z_s.at[d - 1], z_r.at[d - 1], z_peer(d))

    for d in range(1, 8):
        z_copy(d).start()
    uf[...] = pot[...].astype(F32).reshape(EL * 16, 128)

    def half_step(i, carry):
        for p in range(2):
            mine = zh * 4 + i - 1
            u = uf[pl.ds(p * 8 + jnp.clip(mine, 0, 7), EL, stride=16), :]
            W[0, i, p] = jnp.where((mine >= 0) & (mine < 8), u, 0.0).astype(BF16)
            theirs = (1 - zh) * 4 + i - 1
            sr[i, p] = uf[pl.ds(p * 8 + jnp.clip(theirs, 0, 7), EL, stride=16), :].astype(BF16)
        return carry

    lax.fori_loop(0, 6, half_step, 0)
    W[1, 5 * zh] = jnp.zeros((2, EL, 128), BF16)

    @pl.when(s == 0)
    def _():
        H[:, 0] = jnp.zeros((2, 4, EL, 128), BF16)

    @pl.when(s == 15)
    def _():
        H[:, 1] = jnp.zeros((2, 4, EL, 128), BF16)

    start_halo(0)
    def electrodes(i, origin):
        _, lo, n = PIECES[i]
        return pl.ds(pl.multiple_of(origin * EL + lo, 64), n)

    def group(i):
        return e if PIECES[i][0] == 0 else partner

    def field_copy(i, d, part):
        g, lo, n = PIECES[i]
        tx = lax.rem(x + d, 4)
        cols = pl.ds(0, 512) if part == 0 else pl.ds(512, 256)
        return remote(sb.at[g, tx, lo:lo + n, cols], S.at[electrodes(i, group(i)), cols],
                      fs.at[i, part, d - 1], fr.at[i, part, d - 1], x_peer(d))

    def zy_slopes(i):
        g, lo, n = PIECES[i]
        rows = slice(lo, lo + n)
        lane = lax.broadcasted_iota(jnp.int32, (n, 128), 1)

        def step(j, carry):
            t = lax.rem(x + j, 4)
            for p in range(2):
                u = W[g, t + 1, p, rows].astype(F32)
                before, after = W[g, t, p, rows].astype(F32), W[g, t + 2, p, rows].astype(F32)
                left = jnp.where(lane > 0, pltpu.roll(u, 1, axis=1), 0.0)
                right = jnp.where(lane < 127, pltpu.roll(u, 127, axis=1), 0.0)
                sb[g, t, rows, p * 128:p * 128 + 128] = (0.5 * (right - left)).astype(BF16)
                sb[g, t, rows, 256 + p * 128:256 + p * 128 + 128] = (0.5 * (after - before)).astype(BF16)

            @pl.when(j < 4)
            def _():
                field_copy(i, j, 0).start()

            return carry

        lax.fori_loop(1, 5, step, 0)

    def x_slopes(i):
        g, lo, n = PIECES[i]
        rows = slice(lo, lo + n)

        def step(j, carry):
            t = lax.rem(x + j, 4)
            u0, u1 = W[g, t + 1, 0, rows].astype(F32), W[g, t + 1, 1, rows].astype(F32)
            low, high = H[g, 0, t, rows].astype(F32), H[g, 1, t, rows].astype(F32)
            sb[g, t, rows, 512:640] = (0.5 * (u1 - low)).astype(BF16)
            sb[g, t, rows, 640:768] = (0.5 * (high - u0)).astype(BF16)

            @pl.when(j < 4)
            def _():
                field_copy(i, j, 1).start()

            return carry

        lax.fori_loop(1, 5, step, 0)
        S[electrodes(i, group(i)), :] = sb[g, x, rows]

    def forward(i, d):
        origin = (zh if PIECES[i][0] == 0 else 1 - zh) * 8 + lax.rem(x + 4 - d, 4) * 2 + c
        rows = electrodes(i, origin)
        return remote(S.at[rows], S.at[rows], ws.at[i, d], wr.at[i, d], other_core)

    def slab(a, b):
        return pl.ds(pl.multiple_of((a * 4 + b) * ROWS, 16), ROWS)

    def slab_copy(d):
        a = Tb.at[:, slab(y, x)]
        return remote(a, a, p2_s.at[d - 1], p2_r.at[d - 1], x_peer(d))

    def wide_copy(d, dy):
        a = Tb.at[:, slab(y, lax.rem(x + 4 - d, 4))]
        return remote(a, a, p3_s.at[d, dy - 1], p3_r.at[d, dy - 1], y_peer(dy))

    def relay_copy(d, half):
        a = Tb.at[half * 4:half * 4 + 4, slab(lax.rem(y + (3, 1)[half], 4), lax.rem(x + 4 - d, 4))]
        return remote(a, a, p4_s.at[d, half], p4_r.at[d, half], y_peer((1, 3)[half]))

    def relay(d):
        for half, dy in ((0, 1), (1, 3)):
            wide_copy(d, dy).wait_recv()
            relay_copy(d, half).start()

    def pass_on(i, d):
        field_copy(i, d, 0).wait_recv()
        field_copy(i, d, 1).wait_recv()
        forward(i, d).start()

    def start_all(copies):
        for copy in copies:
            copy.start()

    def arrived(copies):
        for copy in copies:
            copy.wait_recv()

    arrived(z_copy(d) for d in range(1, 8))
    raw_copy(1).start()
    raw_copy(2).start()
    start_all(slab_copy(d) for d in (1, 3, 2))
    zy_slopes(0)
    halo_arrived(0)
    x_slopes(0)
    forward(0, 0).start()
    start_all(wide_copy(0, dy) for dy in (1, 3))
    slab_copy(1).wait_recv()
    start_all(wide_copy(1, dy) for dy in (1, 3))
    raw_copy(1).wait_recv()
    start_halo(1)
    zy_slopes(1)
    relay(0)
    slab_copy(3).wait_recv()
    start_all(wide_copy(3, dy) for dy in (1, 3))
    halo_arrived(1)
    x_slopes(1)
    forward(1, 0).start()
    relay(1)
    raw_copy(2).wait_recv()
    start_halo(2)
    zy_slopes(2)
    slab_copy(2).wait_recv()
    start_all(wide_copy(2, dy) for dy in (1, 3))
    halo_arrived(2)
    x_slopes(2)
    forward(2, 0).start()
    relay(3)
    for d in (1, 3, 2):
        pass_on(0, d)
    relay(2)
    for i in (1, 2):
        for d in (1, 3, 2):
            pass_on(i, d)
    for i in range(3):
        arrived(forward(i, d) for d in range(4))

    def product(jj, k, acc):
        rows = pl.ds(pl.multiple_of(k * 4 * ROWS, 16), 4 * ROWS)
        lhs = jnp.concatenate([Tb[2 * jj, rows], Tb[2 * jj + 1, rows]], axis=1)
        first = (c * 4 + jj) * 256
        for n in range(3):
            cols = slice(n * 256, n * 256 + 256)
            image = jnp.dot(lhs, S[pl.ds(pl.multiple_of(first, 256), 256), cols], preferred_element_type=F32)
            for b in range(5):
                own_rows = pl.ds(pl.multiple_of((first + k * 4 * ROWS + b * 64) & (E - 1), 64), 64)
                prod = image[b * 64:b * 64 + 64] * S[own_rows, cols].astype(F32)
                acc = acc + jnp.sum(prod.reshape(8, 8, 256), axis=0)
        return acc

    total = jnp.zeros((8, 256), F32)
    for d in (0, 1, 3, 2):
        if d == 2:
            arrived(relay_copy(o, half) for o in range(4) for half in range(2))
        total = lax.fori_loop(0, 4, lambda jj, acc: product(jj, lax.rem(y + 4 - d, 4), acc), total)
    total = jnp.sum(total, axis=0, keepdims=True)
    gs[...] = jnp.zeros((8, 128), F32)
    gs[0:1, :] = total[:, 0:128]
    gs[1:2, :] = total[:, 128:256]

    cores = remote(gs, gx, c_s, c_r, other_core)
    cores.start()
    cores.wait_recv()
    gt[...] = gs[...] + gx[...]

    def share(k):
        return remote(gt, gr.at[mi], g_s.at[k - 1], g_r.at[k - 1], chip_peer(k))

    for k in range(1, 8):
        share(k).start()
    gr[mi] = gt[...]
    for k in range(1, 8):
        share(k).wait_recv()
    for m in range(8):
        for p in range(2):
            out[p, m:m + 1, :] = gr[m, p:p + 1, :] * weight[p, m:m + 1, :]

    sent = [raw_copy(1), raw_copy(2)]
    for i in range(3):
        halo_sent(i)
        sent += [field_copy(i, d, part) for d in range(1, 4) for part in range(2)]
        sent += [forward(i, d) for d in range(4)]
    sent += [z_copy(d) for d in range(1, 8)]
    for d in range(1, 4):
        sent += [slab_copy(d)]
    for o in range(4):
        sent += [wide_copy(o, dy) for dy in (1, 3)] + [relay_copy(o, half) for half in range(2)]
    sent += [cores] + [share(k) for k in range(1, 8)]
    for copy in sent:
        copy.wait_send()


def local(potentials, quadrupoles, residuals, cell_weight):
    dma = pltpu.SemaphoreType.DMA
    return pl.pallas_call(
        kernel,
        name="misfit_gradient",
        out_shape=jax.ShapeDtypeStruct(cell_weight.shape, F32),
        in_specs=[pl.BlockSpec(memory_space=pltpu.VMEM)] * 4,
        out_specs=pl.BlockSpec(memory_space=pltpu.VMEM),
        scratch_shapes=[
            pltpu.VMEM((EL * 16, 128), F32),
            pltpu.VMEM((2, 6, 2, EL, 128), BF16),
            pltpu.VMEM((6, 2, EL, 128), BF16),
            pltpu.VMEM((2, 2, 4, EL, 128), BF16),
            pltpu.VMEM((2, 4, EL, NC), BF16),
            pltpu.VMEM((E, NC), BF16),
            pltpu.VMEM((8, WIN, 128), BF16),
            pltpu.VMEM((8, 128), F32),
            pltpu.VMEM((8, 128), F32),
            pltpu.VMEM((8, 128), F32),
            pltpu.VMEM((8, 8, 128), F32),
            dma((2,)), dma((2,)),
            dma((3, 2)), dma((3, 2)),
            dma((3, 2, 3)), dma((3, 2, 3)),
            dma((3, 4)), dma((3, 4)),
            dma((7,)), dma((7,)),
            dma((3,)), dma((3,)),
            dma((4, 3)), dma((4, 3)),
            dma((4, 2)), dma((4, 2)),
            dma(()), dma(()),
            dma((7,)), dma((7,)),
        ],
        compiler_params=pltpu.CompilerParams(
            collective_id=0, has_side_effects=True, vmem_limit_bytes=56 << 20),
    )(potentials, quadrupoles, residuals.reshape(1, QUADS), cell_weight)


def solution(mesh):
    placed = (P("elec", "space", None, None), P(), P(), P("space", None, None))
    return jax.shard_map(
        local, mesh=mesh, in_specs=placed, out_specs=P("space", None, None), check_vma=False
    )
```

time: 72.5 us -> 68.4 us (0.943); the launches traced: 71.1 us -> 68.2 us
  Pallas kernels: 69.8 us -> 66.9 us
    pallas_call x1, Pallas kernels: 69.8 us -> 66.9 us  [local(): pl.pallas_call(kernel, name='misfit_gradient', out_shape=jax.ShapeDtypeSt...]
where the time goes in v3:
time: 68.4 us; the launch traced here: 68.2 us
  Pallas kernels  66.9 us (98%)
  local copies, waits for them, and re-layouts  1.3 us (2%)
    pallas_call x1, Pallas kernels, local(): pl.pallas_call(kernel, name='misfit_gradient', out_shape=jax.ShapeDtypeSt...  66.9 us

profile of v3, /device:TPU:32, one launch (start us, length us, event | category | flops | bytes accessed | tf_op | source)
XLA Modules:
  0.0 68.2 jit_solution(6926542149676756618)
XLA Ops:
  0.0 66.9 %misfit_gradient.1 = f32[2,8,128]{2,1,0:T(8,128)} custom-call(bf16[128,2,8,128]{3,2,1,0:T(8,128)(2,1)} %pot.1, s32[4,32768]{1,0:T(4,128)} %quad.1, f32[1,32768]{1,0:T(1,128)} %bitcast.1, f32[2,8,128]{2,1,0:T(8,128)} %weight.1), custom_call_target="tpu_custom_call" | custom-call | tf_op jit(solution)/shard_map/misfit_gradient/pallas_call | solution.py:358
  66.9 1.3 %copy.6 = f32[2,8,128]{2,1,0:T(8,128)} copy(f32[2,8,128]{2,1,0:T(8,128)} %misfit_gradient.1) | data formatting | bytes 16384

commit v4 on v3

--- a/solution.py
+++ b/solution.py
@@ -139,7 +139,7 @@
     def z_copy(d):
         return remote(Tb.at[z, own], Tb.at[z, own], z_s.at[d - 1], z_r.at[d - 1], z_peer(d))
 
-    for d in range(1, 8):
+    for d in (4, 3, 5, 2, 6, 1, 7):
         z_copy(d).start()
     uf[...] = pot[...].astype(F32).reshape(EL * 16, 128)
 
@@ -263,26 +263,26 @@
     raw_copy(1).start()
     raw_copy(2).start()
     start_all(slab_copy(d) for d in (1, 3, 2))
+    start_all(wide_copy(0, dy) for dy in (1, 3))
     zy_slopes(0)
     halo_arrived(0)
     x_slopes(0)
     forward(0, 0).start()
-    start_all(wide_copy(0, dy) for dy in (1, 3))
     slab_copy(1).wait_recv()
     start_all(wide_copy(1, dy) for dy in (1, 3))
     raw_copy(1).wait_recv()
     start_halo(1)
     zy_slopes(1)
-    relay(0)
     slab_copy(3).wait_recv()
     start_all(wide_copy(3, dy) for dy in (1, 3))
+    relay(0)
     halo_arrived(1)
     x_slopes(1)
     forward(1, 0).start()
-    relay(1)
     raw_copy(2).wait_recv()
     start_halo(2)
     zy_slopes(2)
+    relay(1)
     slab_copy(2).wait_recv()
     start_all(wide_copy(2, dy) for dy in (1, 3))
     halo_arrived(2)
@@ -329,7 +329,7 @@
     def share(k):
         return remote(gt, gr.at[mi], g_s.at[k - 1], g_r.at[k - 1], chip_peer(k))
 
-    for k in range(1, 8):
+    for k in (4, 3, 5, 2, 6, 1, 7):
         share(k).start()
     gr[mi] = gt[...]
     for k in range(1, 8):

time: 68.4 us -> 66.3 us (0.969)
  Pallas kernels: 66.9 us -> 64.8 us
    pallas_call x1, Pallas kernels: 66.9 us -> 64.8 us  [local(): pl.pallas_call(kernel, name='misfit_gradient', out_shape=jax.ShapeDtypeSt...]
where the time goes in v4:
time: 66.3 us; the launch traced here: 66.2 us
  Pallas kernels  64.8 us (98%)
  local copies, waits for them, and re-layouts  1.3 us (2%)
    pallas_call x1, Pallas kernels, local(): pl.pallas_call(kernel, name='misfit_gradient', out_shape=jax.ShapeDtypeSt...  64.8 us

profile of v4, /device:TPU:32, one launch (start us, length us, event | category | flops | bytes accessed | tf_op | source)
XLA Modules:
  0.0 66.2 jit_solution(4466371393028427357)
XLA Ops:
  0.0 64.8 %misfit_gradient.1 = f32[2,8,128]{2,1,0:T(8,128)} custom-call(bf16[128,2,8,128]{3,2,1,0:T(8,128)(2,1)} %pot.1, s32[4,32768]{1,0:T(4,128)} %quad.1, f32[1,32768]{1,0:T(1,128)} %bitcast.1, f32[2,8,128]{2,1,0:T(8,128)} %weight.1), custom_call_target="tpu_custom_call" | custom-call | tf_op jit(solution)/shard_map/misfit_gradient/pallas_call | solution.py:358
  64.9 1.3 %copy.6 = f32[2,8,128]{2,1,0:T(8,128)} copy(f32[2,8,128]{2,1,0:T(8,128)} %misfit_gradient.1) | data formatting | bytes 16384

commit v5 on v4

--- a/solution.py
+++ b/solution.py
@@ -14,7 +14,7 @@
 QK = 4096
 ROWS = 80
 WIN = 1280
-PIECES = ((0, 0, 128), (1, 0, 64), (1, 64, 64))
+PIECES = ((0, 0, 128), (1, 0, 128))
 NC = 768
 
 
@@ -261,41 +261,33 @@
 
     arrived(z_copy(d) for d in range(1, 8))
     raw_copy(1).start()
-    raw_copy(2).start()
     start_all(slab_copy(d) for d in (1, 3, 2))
     start_all(wide_copy(0, dy) for dy in (1, 3))
+    slab_copy(1).wait_recv()
+    start_all(wide_copy(1, dy) for dy in (1, 3))
     zy_slopes(0)
     halo_arrived(0)
     x_slopes(0)
     forward(0, 0).start()
-    slab_copy(1).wait_recv()
-    start_all(wide_copy(1, dy) for dy in (1, 3))
+    slab_copy(3).wait_recv()
+    start_all(wide_copy(3, dy) for dy in (1, 3))
     raw_copy(1).wait_recv()
     start_halo(1)
     zy_slopes(1)
-    slab_copy(3).wait_recv()
-    start_all(wide_copy(3, dy) for dy in (1, 3))
-    relay(0)
+    slab_copy(2).wait_recv()
+    start_all(wide_copy(2, dy) for dy in (1, 3))
     halo_arrived(1)
     x_slopes(1)
     forward(1, 0).start()
-    raw_copy(2).wait_recv()
-    start_halo(2)
-    zy_slopes(2)
+    relay(0)
     relay(1)
-    slab_copy(2).wait_recv()
-    start_all(wide_copy(2, dy) for dy in (1, 3))
-    halo_arrived(2)
-    x_slopes(2)
-    forward(2, 0).start()
     relay(3)
     for d in (1, 3, 2):
         pass_on(0, d)
     relay(2)
-    for i in (1, 2):
-        for d in (1, 3, 2):
-            pass_on(i, d)
-    for i in range(3):
+    for d in (1, 3, 2):
+        pass_on(1, d)
+    for i in range(2):
         arrived(forward(i, d) for d in range(4))
 
     def product(jj, k, acc):
@@ -338,8 +330,8 @@
         for p in range(2):
             out[p, m:m + 1, :] = gr[m, p:p + 1, :] * weight[p, m:m + 1, :]
 
-    sent = [raw_copy(1), raw_copy(2)]
-    for i in range(3):
+    sent = [raw_copy(1)]
+    for i in range(2):
         halo_sent(i)
         sent += [field_copy(i, d, part) for d in range(1, 4) for part in range(2)]
         sent += [forward(i, d) for d in range(4)]

time: 66.3 us -> 62.6 us (0.944); the launches traced: 66.2 us -> 61.4 us
  Pallas kernels: 64.8 us -> 60.1 us
    pallas_call x1, Pallas kernels: 64.8 us -> 60.1 us  [local(): pl.pallas_call(kernel, name='misfit_gradient', out_shape=jax.ShapeDtypeSt...]
where the time goes in v5:
time: 62.6 us; the launch traced here: 61.4 us
  Pallas kernels  60.1 us (96%)
  local copies, waits for them, and re-layouts  1.3 us (2%)
    pallas_call x1, Pallas kernels, local(): pl.pallas_call(kernel, name='misfit_gradient', out_shape=jax.ShapeDtypeSt...  60.1 us
    unnamed x1, local copies, waits for them, and re-layouts  1.3 us

profile of v5, /device:TPU:32, one launch (start us, length us, event | category | flops | bytes accessed | tf_op | source)
XLA Modules:
  0.0 61.4 jit_solution(12923695429857111049)
XLA Ops:
  0.0 60.1 %misfit_gradient.1 = f32[2,8,128]{2,1,0:T(8,128)} custom-call(bf16[128,2,8,128]{3,2,1,0:T(8,128)(2,1)} %pot.1, s32[4,32768]{1,0:T(4,128)} %quad.1, f32[1,32768]{1,0:T(1,128)} %bitcast.1, f32[2,8,128]{2,1,0:T(8,128)} %weight.1), custom_call_target="tpu_custom_call" | custom-call | tf_op jit(solution)/shard_map/misfit_gradient/pallas_call | solution.py:350
  60.1 1.3 %copy.6 = f32[2,8,128]{2,1,0:T(8,128)} copy(f32[2,8,128]{2,1,0:T(8,128)} %misfit_gradient.1) | data formatting | bytes 16384

commit v6 on v5

--- a/solution.py
+++ b/solution.py
@@ -271,11 +271,11 @@
     forward(0, 0).start()
     slab_copy(3).wait_recv()
     start_all(wide_copy(3, dy) for dy in (1, 3))
+    slab_copy(2).wait_recv()
+    start_all(wide_copy(2, dy) for dy in (1, 3))
     raw_copy(1).wait_recv()
     start_halo(1)
     zy_slopes(1)
-    slab_copy(2).wait_recv()
-    start_all(wide_copy(2, dy) for dy in (1, 3))
     halo_arrived(1)
     x_slopes(1)
     forward(1, 0).start()

time: 62.6 us -> 61.8 us (0.987); the launches traced: 61.4 us -> 61.4 us
  no operation moved by 1% of the time
where the time goes in v6:
time: 61.8 us; the launch traced here: 61.4 us
  Pallas kernels  60.1 us (97%)
  local copies, waits for them, and re-layouts  1.3 us (2%)
    pallas_call x1, Pallas kernels, local(): pl.pallas_call(kernel, name='misfit_gradient', out_shape=jax.ShapeDtypeSt...  60.1 us
    unnamed x1, local copies, waits for them, and re-layouts  1.3 us

profile of v6, /device:TPU:32, one launch (start us, length us, event | category | flops | bytes accessed | tf_op | source)
XLA Modules:
  0.0 61.4 jit_solution(18132694643277700788)
XLA Ops:
  0.0 60.1 %misfit_gradient.1 = f32[2,8,128]{2,1,0:T(8,128)} custom-call(bf16[128,2,8,128]{3,2,1,0:T(8,128)(2,1)} %pot.1, s32[4,32768]{1,0:T(4,128)} %quad.1, f32[1,32768]{1,0:T(1,128)} %bitcast.1, f32[2,8,128]{2,1,0:T(8,128)} %weight.1), custom_call_target="tpu_custom_call" | custom-call | tf_op jit(solution)/shard_map/misfit_gradient/pallas_call | solution.py:350
  60.1 1.3 %copy.6 = f32[2,8,128]{2,1,0:T(8,128)} copy(f32[2,8,128]{2,1,0:T(8,128)} %misfit_gradient.1) | data formatting | bytes 16384
